TPU v7x, 128 devices: a whole 4x4x4 slice. The times are simulated.
128 devices in a mesh: dp: 8 (over y, core), queue: 16 (over z, x).
Axes of the slice: x: 4, y: 4, z: 4, core: 2. Of those that a mesh axis runs over, the one named last changes fastest.
Arguments:
- queue_keys: bfloat16 [524288, 768], P(('dp', 'queue')), may hold values from -2.5 to 2.5
- fresh_keys: bfloat16 [1024, 768], P(('dp', 'queue')), may hold values from -4 to 4
- slots: int32 [1024], P(('dp', 'queue')), may hold values from 0 to 524287, as said below
- queries: bfloat16 [1024, 768], P('dp'), may hold values from -40 to 40
- positives: int32 [1024], P('dp'), may hold values from 0 to 1023
Outputs:
- query_grad: float32 [1024, 768], P(('dp', 'queue'))
- mean_loss: float32 [], replicated
- new_queue: bfloat16 [524288, 768], P(('dp', 'queue'))
Inputs may be any that keep to these rules, and one draw needn't show every extreme that they name: The 1024 slots are distinct.
All inputs are finite; a program needn't handle non-finite values.
Results may differ from a plain program's by a relative error of at most 0.0035.
Values may be sent and summed in bfloat16 or wider, within the bound.
A program may use at most 128 MiB of HBM per device.

v0:
```python
import jax
import jax.numpy as jnp
from jax import lax
from jax.sharding import PartitionSpec as P


def score_rows(query_rows, key_rows):
    return lax.dot_general(
        query_rows, key_rows, (((1,), (1,)), ((), ())), preferred_element_type=jnp.float32
    )


def shards(queue_keys, fresh_keys, slots, queries, positives):
    all_queries = lax.all_gather(queries, "dp", axis=0, tiled=True)
    fresh_all, slots_all = (
        lax.all_gather(fresh_keys, ("dp", "queue"), axis=0, tiled=True),
        lax.all_gather(slots, ("dp", "queue"), axis=0, tiled=True),
    )
    queue_scores = score_rows(all_queries, queue_keys)
    fresh_scores = score_rows(all_queries, fresh_keys)
    local_top = jnp.maximum(jnp.max(queue_scores, axis=1), jnp.max(fresh_scores, axis=1))
    row_top = lax.pmax(local_top, ("dp", "queue"))
    queue_exp = jnp.exp(queue_scores - row_top[:, None])
    fresh_exp = jnp.exp(fresh_scores - row_top[:, None])
    local_sum = jnp.sum(queue_exp, axis=1) + jnp.sum(fresh_exp, axis=1)
    sum_exp = lax.psum(local_sum, ("dp", "queue"))
    queue_weights = queue_exp.astype(jnp.bfloat16)
    fresh_weights = fresh_exp.astype(jnp.bfloat16)
    dp_size = lax.axis_size("dp")
    queue_size = lax.axis_size("queue")
    own_rows = all_queries.shape[0] // (dp_size * queue_size)
    pulled = lax.psum_scatter(
        jnp.dot(queue_weights, queue_keys, preferred_element_type=jnp.float32)
        + jnp.dot(fresh_weights, fresh_keys, preferred_element_type=jnp.float32),
        ("dp", "queue"),
        scatter_dimension=0,
        tiled=True,
    )
    queue_index = lax.axis_index("queue")
    device_index = lax.axis_index("dp") * queue_size + queue_index
    row_start = device_index * own_rows
    top_rows = lax.dynamic_slice_in_dim(row_top, row_start, own_rows, 0)
    total_rows = lax.dynamic_slice_in_dim(sum_exp, row_start, own_rows, 0)
    local_start = queue_index * own_rows
    positive_rows = lax.dynamic_slice_in_dim(positives, local_start, own_rows, 0)
    query_rows = lax.dynamic_slice_in_dim(queries, local_start, own_rows, 0)
    positive_keys = jnp.take(fresh_all, positive_rows, axis=0).astype(jnp.float32)
    query_grad = pulled / total_rows[:, None] - positive_keys
    positive_scores = jnp.sum(query_rows.astype(jnp.float32) * positive_keys, axis=1)
    loss_part = jnp.sum(top_rows + jnp.log(total_rows) - positive_scores)
    loss_sum = lax.psum(loss_part, ("dp", "queue"))
    mean_loss = loss_sum / (own_rows * dp_size * queue_size)
    held_rows = queue_keys.shape[0]
    local_slot = slots_all - device_index * held_rows
    inside = (local_slot >= 0) & (local_slot < held_rows)
    target = jnp.where(inside, local_slot, held_rows)
    new_queue = queue_keys.at[target].set(fresh_all, mode="drop")
    return (query_grad, mean_loss, new_queue)


def solution(mesh):
    placed = (
        P(("dp", "queue"), None),
        P(("dp", "queue"), None),
        P(("dp", "queue")),
        P("dp", None),
        P("dp"),
    )
    return jax.shard_map(
        shards,
        mesh=mesh,
        in_specs=placed,
        out_specs=(P(("dp", "queue"), None), P(), P(("dp", "queue"), None)),
        check_vma=False,
    )
```

profile of v0, /device:TPU:1, one launch (start us, length us, event | category | flops | bytes accessed | tf_op | source)
XLA Modules:
  0.0 360.9 jit_solution(16796866037747466775)
XLA Ops:
  7.2 0.0 all-gather.3.cloned.1.call-start
  7.2 5.9 %copy.11 = bf16[4096,768]{1,0:T(8,128)(2,1)} copy(bf16[4096,768]{1,0:T(8,128)(2,1)} %param.5) | data formatting | bytes 12582912
  13.1 0.0 all-gather.3.cloned.1.call-update
  13.1 0.0 all-gather.5.cloned.1.call-start
  13.2 0.7 all-gather.5.cloned.1.call-update
  13.9 0.0 reduce-scatter.2.cloned.1.call-start
  13.9 27.3 %all-gather.3.cloned.1.call-done = bf16[1024,768]{1,0:T(8,128)(2,1)} async-done(((bf16[128,768]{1,0:T(8,128)(2,1)}), bf16[1024,768]{1,0:T(8,128)(2,1)}) %all-gather.3.cloned.1.call-update) | async-done | bytes 1572880 | tf_op jit(solution)/shard_map/all_gather | solution.py:14
  41.3 13.3 %fusion.10 = (f32[1024]{0:T(1024)S(1)}, f32[1024,4096]{1,0:T(8,128)}) fusion(bf16[1024,768]{1,0:T(8,128)(2,1)} %all-gather.3.cloned.1.call-done, bf16[4096,768]{1,0:T(8,128)(2,1)} %copy.11), kind=kOutput, calls=%fused_computation.21 | convolution fusion | flops 6446644224 | bytes 24645632 | tf_op jit(solution)/shard_map/dot_general | solution.py:8
  54.6 0.5 fusion.11
  55.1 64.9 %pmax.7 = f32[1024]{0:T(1024)S(1)} all-reduce(f32[1024]{0:T(1024)S(1)} %max.5), channel_id=1, replica_groups=mesh['dp'=8,'queue'=16] {'dp','queue'}, use_global_device_ids=true, to_apply=%region_2.0 | all-reduce | flops 1024 | bytes 8192 | tf_op jit(solution)/shard_map/pmax | solution.py:22
  120.1 12.3 %fusion.2 = f32[1024,768]{1,0:T(8,128)S(1)} fusion(bf16[4096,768]{1,0:T(8,128)(2,1)} %copy.11, f32[1024,4096]{1,0:T(8,128)} %get-tuple-element.8, f32[1024]{0:T(1024)S(1)} %pmax.7), kind=kOutput, calls=%fused_computation.5 | convolution fusion | flops 6450839552 | bytes 26218496 | tf_op jit(solution)/shard_map/dot_general | solution.py:33
  132.4 2.3 convolution_add_fusion
  134.7 0.0 reduce-scatter.2.cloned.1.call-update
  134.7 0.2 dynamic-update-slice
  135.0 64.1 %all-reduce = s32[1024]{0:T(1024)S(1)} all-reduce(s32[1024]{0:T(1024)S(1)} %dynamic-update-slice), channel_id=1, replica_groups=mesh['dp'=8,'queue'=16] {'dp','queue'}, use_global_device_ids=true, to_apply=%add | all-reduce | flops 1024 | bytes 8192
  199.1 0.1 compare_and_fusion
  199.2 8.2 %fusion = f32[1024]{0:T(1024)S(1)} fusion(f32[1024,4096]{1,0:T(8,128)} %get-tuple-element.8, f32[1024]{0:T(1024)S(1)} %pmax.7), kind=kLoop, calls=%fused_computation.3 | loop fusion | flops 8387584 | bytes 16785408 | tf_op jit(solution)/shard_map/reduce_sum | solution.py:25
  207.4 62.7 %psum.14 = f32[1024]{0:T(1024)S(1)} all-reduce(f32[1024]{0:T(1024)S(1)} %add.34), channel_id=1, replica_groups=mesh['dp'=8,'queue'=16] {'dp','queue'}, use_global_device_ids=true, to_apply=%region_6.0 | all-reduce | flops 1024 | bytes 8192 | tf_op jit(solution)/shard_map/psum | solution.py:26
  270.2 2.2 gather_fusion
  272.4 0.9 fusion.7
  273.3 0.7 subtract_reduce_fusion
  273.9 64.7 %psum.15 = f32[]{:T(128)} all-reduce(f32[]{:T(128)} %get-tuple-element.3), channel_id=1, replica_groups=mesh['dp'=8,'queue'=16] {'dp','queue'}, use_global_device_ids=true, to_apply=%region_9.10 | all-reduce | flops 1 | bytes 8 | tf_op jit(solution)/shard_map/psum | solution.py:51
  339.3 12.4 %scatter_fusion = bf16[4096,768]{1,0:T(8,128)(2,1)} fusion(bf16[4096,768]{1,0:T(8,128)(2,1)} %copy.11, s32[1024]{0:T(1024)S(1)} %compare_select_fusion, bf16[1024,768]{1,0:T(8,128)(2,1)} %all-gather.5.cloned.1.call-done), kind=kCustom, calls=%fused_computation.1 | custom fusion | bytes 4722688 | tf_op jit(solution)/shard_map/scatter | solution.py:57
  351.8 1.4 convert_subtract_fusion
  (16 shorter events, 0.1 us)
Async XLA Ops:
  7.2 34.1 %all-gather.3.cloned.1.call-start = ((), (), s32[]{:S(2)}) async-start(), calls=%async_computation.1 | async-start | bytes 1769472 | tf_op jit(solution)/shard_map/all_gather | solution.py:14
  13.1 257.0 %all-gather.5.cloned.1.call-start = ((), (), s32[]{:S(2)}) async-start(), calls=%async_computation.3 | async-start | bytes 1585152 | tf_op jit(solution)/shard_map/all_gather | solution.py:16
  13.9 40.7 %copy-start.1 = (bf16[8,768]{1,0:T(8,128)(2,1)S(1)}, bf16[8,768]{1,0:T(8,128)(2,1)}, u32[]{:S(2)}) copy-start(bf16[8,768]{1,0:T(8,128)(2,1)} %param.6) | copy-start | bytes 36868
  13.9 337.9 %reduce-scatter.2.cloned.1.call-start = ((), (), s32[]{:S(2)}) async-start(), calls=%async_computation.2 | async-start | bytes 3170304 | tf_op jit(solution)/shard_map/reduce_scatter | solution.py:32
  41.3 13.3 %copy-start = (bf16[1024,768]{1,0:T(8,128)(2,1)S(1)}, bf16[1024,768]{1,0:T(8,128)(2,1)}, u32[]{:S(2)}) copy-start(bf16[1024,768]{1,0:T(8,128)(2,1)} %all-gather.3.cloned.1.call-done) | copy-start | bytes 4718596
  132.3 2.4 copy-start.3
  132.4 66.7 %copy-start.2 = (s32[128]{0:T(128)S(1)}, s32[128]{0:T(128)}, u32[]{:S(2)}) copy-start(s32[128]{0:T(128)} %param.9) | copy-start | bytes 1540
Sparse Core Ops, SparseCore 0:
  13.2 27.9 all-gather.2
  44.0 64.3 all-gather.4
  134.8 205.3 reduce-scatter.1
where the time goes:
time: 362 us; the launch traced here: 361 us
  blocking collectives  256 us (71%)
  matrix products  28.4 us (8%)
  waiting for transfers between devices  28 us (8%)
  local copies, waits for them, and re-layouts  20.8 us (6%)
  between operations  15.6 us (4%)
  other arithmetic  11.4 us (3%)
    pmax x1, blocking collectives, shards(): row_top = lax.pmax(local_top, ('dp', 'queue'))  64.9 us
    psum x1, blocking collectives, shards(): loss_sum = lax.psum(loss_part, ('dp', 'queue'))  64.7 us
    unnamed x1, blocking collectives  64.1 us
    psum x1, blocking collectives, shards(): sum_exp = lax.psum(local_sum, ('dp', 'queue'))  62.7 us
    all_gather x1, waiting for transfers between devices, shards(): all_queries = lax.all_gather(queries, 'dp', axis=0, tiled=True)  27.3 us
    dot_general x2, matrix products, score_rows(): lax.dot_general(query_rows, key_rows, (((1,), (1,)), ((), ())), preferred...  13.8 us
    scatter x1, local copies, waits for them, and re-layouts, shards(): new_queue = queue_keys.at[target].set(fresh_all, mode='drop')  12.4 us
    dot_general x1, matrix products, shards(): jnp.dot(queue_weights, queue_keys, preferred_element_type=jnp.float32)  12.3 us
  transfers between devices with their start and end apart: 3, of which 1 were waited for; matrix products, arithmetic and copies ran while one was open for 15% of the time, Pallas kernels for 0%

commit v1 on v0

--- a/solution.py
+++ b/solution.py
@@ -23,7 +23,8 @@
     queue_exp = jnp.exp(queue_scores - row_top[:, None])
     fresh_exp = jnp.exp(fresh_scores - row_top[:, None])
     local_sum = jnp.sum(queue_exp, axis=1) + jnp.sum(fresh_exp, axis=1)
-    sum_exp = lax.psum(local_sum, ("dp", "queue"))
+    parts = lax.all_gather(local_sum, ("dp", "queue"))
+    sum_exp = jnp.sum(parts, axis=0)
     queue_weights = queue_exp.astype(jnp.bfloat16)
     fresh_weights = fresh_exp.astype(jnp.bfloat16)
     dp_size = lax.axis_size("dp")

time: 362 us -> 351 us (0.970)
  blocking collectives: 256 us -> 244 us
    psum x1 -> x0, blocking collectives: 62.7 us -> none  [shards(): sum_exp = lax.psum(local_sum, ('dp', 'queue'))]
    all_gather x0 -> x1, blocking collectives: none -> 50.6 us  [shards(): parts = lax.all_gather(local_sum, ('dp', 'queue'))]
  transfers between devices with their start and end apart: 3 -> 3, of which waited for: 1 -> 2; matrix products, arithmetic and copies ran while one was open for 15% -> 15% of each run, Pallas kernels for 0% -> 0%
where the time goes in v1:
time: 351 us; the launch traced here: 349 us
  blocking collectives  244 us (70%)
  matrix products  28.4 us (8%)
  waiting for transfers between devices  28.2 us (8%)
  local copies, waits for them, and re-layouts  20.9 us (6%)
  between operations  15.7 us (4%)
  other arithmetic  11.4 us (3%)
    pmax x1, blocking collectives, shards(): row_top = lax.pmax(local_top, ('dp', 'queue'))  64.9 us
    psum x1, blocking collectives, shards(): loss_sum = lax.psum(loss_part, ('dp', 'queue'))  64.7 us
    unnamed x1, blocking collectives  64.1 us
    all_gather x1, blocking collectives, shards(): parts = lax.all_gather(local_sum, ('dp', 'queue'))  50.6 us
    all_gather x1, waiting for transfers between devices, shards(): all_queries = lax.all_gather(queries, 'dp', axis=0, tiled=True)  27.3 us
    dot_general x2, matrix products, score_rows(): lax.dot_general(query_rows, key_rows, (((1,), (1,)), ((), ())), preferred...  13.8 us
    scatter x1, local copies, waits for them, and re-layouts, shards(): new_queue = queue_keys.at[target].set(fresh_all, mode='drop')  12.4 us
    dot_general x1, matrix products, shards(): jnp.dot(queue_weights, queue_keys, preferred_element_type=jnp.float32)  12.3 us
  transfers between devices with their start and end apart: 3, of which 2 were waited for; matrix products, arithmetic and copies ran while one was open for 15% of the time, Pallas kernels for 0%

profile of v1, /device:TPU:1, one launch (start us, length us, event | category | flops | bytes accessed | tf_op | source)
XLA Modules:
  0.0 348.9 jit_solution(4218929645868963226)
XLA Ops:
  7.2 0.0 all-gather.4.cloned.1.call-start
  7.2 5.9 %copy.11 = bf16[4096,768]{1,0:T(8,128)(2,1)} copy(bf16[4096,768]{1,0:T(8,128)(2,1)} %param.5) | data formatting | bytes 12582912
  13.1 0.0 all-gather.6.cloned.1.call-start
  13.2 0.7 all-gather.6.cloned.1.call-update
  13.9 0.0 reduce-scatter.2.cloned.1.call-start
  13.9 27.3 %all-gather.4.cloned.1.call-done = bf16[1024,768]{1,0:T(8,128)(2,1)} async-done(((bf16[128,768]{1,0:T(8,128)(2,1)}), bf16[1024,768]{1,0:T(8,128)(2,1)}) %all-gather.4.cloned.1.call-update) | async-done | bytes 1572880 | tf_op jit(solution)/shard_map/all_gather | solution.py:14
  41.3 13.3 %fusion.10 = (f32[1024]{0:T(1024)S(1)}, f32[1024,4096]{1,0:T(8,128)}) fusion(bf16[1024,768]{1,0:T(8,128)(2,1)} %all-gather.4.cloned.1.call-done, bf16[4096,768]{1,0:T(8,128)(2,1)} %copy.11), kind=kOutput, calls=%fused_computation.21 | convolution fusion | flops 6446644224 | bytes 24645632 | tf_op jit(solution)/shard_map/dot_general | solution.py:8
  54.6 0.5 fusion.11
  55.1 64.9 %pmax.7 = f32[1024]{0:T(1024)S(1)} all-reduce(f32[1024]{0:T(1024)S(1)} %max.5), channel_id=1, replica_groups=mesh['dp'=8,'queue'=16] {'dp','queue'}, use_global_device_ids=true, to_apply=%region_2.0 | all-reduce | flops 1024 | bytes 8192 | tf_op jit(solution)/shard_map/pmax | solution.py:22
  120.1 12.3 %fusion.2 = f32[1024,768]{1,0:T(8,128)S(1)} fusion(bf16[4096,768]{1,0:T(8,128)(2,1)} %copy.11, f32[1024,4096]{1,0:T(8,128)} %get-tuple-element.8, f32[1024]{0:T(1024)S(1)} %pmax.7), kind=kOutput, calls=%fused_computation.5 | convolution fusion | flops 6450839552 | bytes 26218496 | tf_op jit(solution)/shard_map/dot_general | solution.py:34
  132.4 2.3 convolution_add_fusion
  134.7 0.2 dynamic-update-slice
  135.0 64.1 %all-reduce = s32[1024]{0:T(1024)S(1)} all-reduce(s32[1024]{0:T(1024)S(1)} %dynamic-update-slice), channel_id=1, replica_groups=mesh['dp'=8,'queue'=16] {'dp','queue'}, use_global_device_ids=true, to_apply=%add | all-reduce | flops 1024 | bytes 8192
  199.1 0.1 compare_and_fusion
  199.2 8.2 %fusion = f32[1024]{0:T(1024)S(1)} fusion(f32[1024,4096]{1,0:T(8,128)} %get-tuple-element.8, f32[1024]{0:T(1024)S(1)} %pmax.7), kind=kLoop, calls=%fused_computation.3 | loop fusion | flops 8387584 | bytes 16785408 | tf_op jit(solution)/shard_map/reduce_sum | solution.py:25
  207.4 50.6 %all-gather = f32[131072]{0:T(1024)S(1)} all-gather(f32[1024]{0:T(1024)S(1)} %add.42), channel_id=2, replica_groups=mesh['dp'=8,'queue'=16] {'dp','queue'}, dimensions={0}, use_global_device_ids=true | all-gather | bytes 528384 | tf_op jit(solution)/shard_map/all_gather | solution.py:26
  258.0 0.1 reshape.41
  258.2 2.2 gather_fusion
  260.4 0.9 fusion.7
  261.3 0.7 subtract_reduce_fusion
  262.0 64.7 %psum.7 = f32[]{:T(128)} all-reduce(f32[]{:T(128)} %get-tuple-element.3), channel_id=1, replica_groups=mesh['dp'=8,'queue'=16] {'dp','queue'}, use_global_device_ids=true, to_apply=%region_9.10 | all-reduce | flops 1 | bytes 8 | tf_op jit(solution)/shard_map/psum | solution.py:52
  327.3 12.4 %scatter_fusion = bf16[4096,768]{1,0:T(8,128)(2,1)} fusion(bf16[4096,768]{1,0:T(8,128)(2,1)} %copy.11, s32[1024]{0:T(1024)S(1)} %compare_select_fusion, bf16[1024,768]{1,0:T(8,128)(2,1)} %all-gather.6.cloned.1.call-done), kind=kCustom, calls=%fused_computation.1 | custom fusion | bytes 4722688 | tf_op jit(solution)/shard_map/scatter | solution.py:58
  339.7 0.1 reduce-scatter.2.cloned.1.call-done
  339.8 1.4 convert_subtract_fusion
  (18 shorter events, 0.2 us)
Async XLA Ops:
  7.2 34.1 %all-gather.4.cloned.1.call-start = ((), (), s32[]{:S(2)}) async-start(), calls=%async_computation.1 | async-start | bytes 1769472 | tf_op jit(solution)/shard_map/all_gather | solution.py:14
  13.1 245.0 %all-gather.6.cloned.1.call-start = ((), (), s32[]{:S(2)}) async-start(), calls=%async_computation.3 | async-start | bytes 1585152 | tf_op jit(solution)/shard_map/all_gather | solution.py:16
  13.9 40.7 %copy-start.1 = (bf16[8,768]{1,0:T(8,128)(2,1)S(1)}, bf16[8,768]{1,0:T(8,128)(2,1)}, u32[]{:S(2)}) copy-start(bf16[8,768]{1,0:T(8,128)(2,1)} %param.6) | copy-start | bytes 36868
  13.9 325.9 %reduce-scatter.2.cloned.1.call-start = ((), (), s32[]{:S(2)}) async-start(), calls=%async_computation.2 | async-start | bytes 3170304 | tf_op jit(solution)/shard_map/reduce_scatter | solution.py:33
  41.3 13.3 %copy-start = (bf16[1024,768]{1,0:T(8,128)(2,1)S(1)}, bf16[1024,768]{1,0:T(8,128)(2,1)}, u32[]{:S(2)}) copy-start(bf16[1024,768]{1,0:T(8,128)(2,1)} %all-gather.4.cloned.1.call-done) | copy-start | bytes 4718596
  132.3 2.4 copy-start.3
  132.4 66.7 %copy-start.2 = (s32[128]{0:T(128)S(1)}, s32[128]{0:T(128)}, u32[]{:S(2)}) copy-start(s32[128]{0:T(128)} %param.9) | copy-start | bytes 1540
Sparse Core Ops, SparseCore 0:
  13.2 27.9 all-gather.3
  44.0 64.3 all-gather.5
  134.8 204.9 reduce-scatter.1
